TPU v7x, 32 devices: a whole 2x2x4 slice. The times are simulated.
32 devices in a mesh: group: 1, tile: 8 (over z, core), dp: 4 (over y, x).
Axes of the slice: x: 2, y: 2, z: 4, core: 2. Of those that a mesh axis runs over, the one named last changes fastest.
Arguments:
- activations: bfloat16 [4, 8, 24, 24, 128], P(('group', 'dp'), 'tile'), may hold values from -6 to 6
- cotangent: bfloat16 [4, 8, 24, 24, 128], P(('group', 'dp'), 'tile'), may hold values from -1.5 to 1.5
- kernel: bfloat16 [1152, 128], P('group'), may hold values from -0.1875 to 0.1875
- turning: int32 [8], P('tile'), may hold values from 0 to 3
- orient: int32 [8, 4], P('tile'), may hold values from 0 to 7, as said below
- left_factor: float32 [1152, 1152], P(('group', 'tile')), may hold values from -0.15 to 5.15
- left_basis: float32 [1152, 1152], P(('group', 'tile'), 'dp'), may hold values from -0.026516504 to 1.0265165
- right_factor: float32 [128, 128], P('group'), may hold values from -4.26 to 49.26
- right_basis: float32 [128, 128], P('group'), may hold values from -0.079549513 to 1.0795495
- momentum: float32 [1152, 128], P(('group', 'dp')), may hold values from -1.5 to 1.5
- second_moment: float32 [1152, 128], P(('group', 'dp')), may hold values from 0.02 to 0.2
Outputs:
- output: bfloat16 [4, 8, 24, 24, 128], P(('group', 'dp'), 'tile')
- input_grad: bfloat16 [4, 8, 24, 24, 128], P(('group', 'dp'), 'tile')
- kernel_grad: float32 [1152, 128], P('group')
- left_factor_new: float32 [1152, 1152], P(('group', 'tile'))
- left_basis_new: float32 [1152, 1152], P(('group', 'tile'))
- right_factor_new: float32 [128, 128], P('group')
- right_basis_new: float32 [128, 128], P('group')
- momentum_new: float32 [1152, 128], P(('group', 'dp'))
- second_new: float32 [1152, 128], P(('group', 'dp'))
- update: float32 [1152, 128], P(('group', 'tile'))
Inputs may be any that keep to these rules, and one draw needn't show every extreme that they name: 0 where edge e of tile t leaves the patch; otherwise orient[t, e] % 4 is the edge of neighbor[t, e] that heads back to t, and 4 is added where the two edges' cell orders run opposite ways.
All inputs are finite; a program needn't handle non-finite values.
Results may differ from a plain program's by a relative error of at most 0.0025.
Values may be sent and summed in bfloat16 or wider, within the bound.
A program may use at most 128 MiB of HBM per device.

v0:
```python
import math
import jax
import jax.numpy as jnp
from jax import lax
from jax.sharding import PartitionSpec as P

highest = lax.Precision.HIGHEST
epsilon = 1e-08


def edge_strips(values):
    return jnp.stack(
        [values[..., 0, :, :], values[..., :, -1, :], values[..., -1, :, :], values[..., :, 0, :]],
        axis=0,
    )


def cycle_strips(spread):
    return jnp.stack(
        [spread[:, 0, 1:-1], spread[:, 1:-1, -1], spread[:, -1, 1:-1], spread[:, 1:-1, 0]], axis=0
    )


def assemble(tile_vals, borders):
    middle = jnp.concatenate(
        [borders[3][:, :, None, :], tile_vals, borders[1][:, :, None, :]], axis=2
    )
    top_row = jnp.pad(borders[0], ((0, 0), (1, 1), (0, 0)))[:, None]
    bottom_row = jnp.pad(borders[2], ((0, 0), (1, 1), (0, 0)))[:, None]
    return jnp.concatenate([top_row, middle, bottom_row], axis=1)


def tap_patches(padded, side):
    pieces = [
        padded[:, row_off : row_off + side, col_off : col_off + side, :]
        for row_off in range(3)
        for col_off in range(3)
    ]
    joined = jnp.concatenate(pieces, axis=-1)
    return joined.reshape(-1, joined.shape[-1])


def spread_back(flat_grads, kernel, sample_count, side):
    channels = kernel.shape[1]
    summed = jnp.zeros((sample_count, side + 2, side + 2, channels), jnp.float32)
    for tap_index in range(9):
        row_off, col_off = divmod(tap_index, 3)
        weight_tap = kernel[tap_index * channels : (tap_index + 1) * channels]
        contrib = lax.dot_general(
            flat_grads, weight_tap, (((1,), (1,)), ((), ())), preferred_element_type=jnp.float32
        )
        contrib = contrib.reshape(sample_count, side, side, channels)
        summed = summed + jnp.pad(
            contrib, ((0, 0), (row_off, 2 - row_off), (col_off, 2 - col_off), (0, 0))
        )
    return summed


def absorb_rims(interior, incoming):
    result = interior.at[..., 0, :, :].add(incoming[0])
    result = result.at[..., :, -1, :].add(incoming[1])
    result = result.at[..., -1, :, :].add(incoming[2])
    return result.at[..., :, 0, :].add(incoming[3])


def flip_edges(strips, flipped):
    return jnp.where(flipped[:, None, None, None], strips[:, :, ::-1, :], strips)


def pick_gathered(everything, near_tiles, facing, flipped, usable):
    flat = everything.reshape(everything.shape[0] * 4, -1)
    wanted = jnp.where(usable, near_tiles * 4 + facing, -1)
    selector = (lax.broadcasted_iota(jnp.int32, (4, flat.shape[0]), 1) == wanted[:, None]).astype(
        jnp.bfloat16
    )
    picked = jnp.dot(selector, flat, preferred_element_type=jnp.float32).astype(jnp.bfloat16)
    return flip_edges(picked.reshape((4,) + everything.shape[2:]), flipped)


def orthonormal(power):
    gram = lax.dot_general(power, power, (((0,), (0,)), ((), ())), precision=highest)
    lower = jnp.linalg.cholesky(gram)
    return lax.linalg.triangular_solve(lower, power.T, left_side=True, lower=True).T


def body(
    activations,
    cotangent,
    kernel,
    turning,
    orient,
    left_factor,
    left_basis,
    right_factor,
    right_basis,
    momentum,
    second_moment,
):
    tiles = lax.axis_size("tile")
    dp_count = lax.axis_size("dp")
    tile_index = lax.axis_index("tile")
    dp_index = lax.axis_index("dp")
    tile_vals = activations[:, 0]
    tile_grads = cotangent[:, 0]
    sample_count = tile_vals.shape[0]
    side = tile_vals.shape[1]
    channels = tile_vals.shape[-1]
    own_turn = turning[0]
    facing = orient[0] % 4
    flipped = orient[0] >= 4
    heading = (jnp.arange(4, dtype=jnp.int32) + own_turn) % 4
    row_of = tile_index // 4
    col_of = tile_index % 4
    room = jnp.stack([row_of > 0, col_of < 3, row_of < tiles // 4 - 1, col_of > 0])
    usable = (
        jnp.sum(
            jnp.where(
                heading[:, None] == jnp.arange(4, dtype=jnp.int32)[None, :], room[None, :], False
            ),
            axis=1,
        )
        > 0
    )
    offsets = jnp.array([-4, 1, 4, -1], dtype=jnp.int32)
    near_tiles = tile_index + jnp.sum(
        jnp.where(heading[:, None] == jnp.arange(4, dtype=jnp.int32)[None, :], offsets[None, :], 0),
        axis=1,
    )
    strips = edge_strips(tile_vals)
    everything = lax.all_gather(strips[None], "tile", axis=0, tiled=True)
    borders = pick_gathered(everything, near_tiles, facing, flipped, usable)
    padded = assemble(tile_vals, borders)
    columns = tap_patches(padded, side)
    flat_grads = tile_grads.reshape(-1, channels)
    partial_grad = lax.dot_general(
        columns, flat_grads, (((0,), (0,)), ((), ())), preferred_element_type=jnp.float32
    )
    summed_grad = lax.psum(partial_grad, ("tile", "dp"))
    result = jnp.dot(columns, kernel, preferred_element_type=jnp.float32).astype(jnp.bfloat16)
    result = result.reshape(activations.shape)
    spread = spread_back(flat_grads, kernel, sample_count, side)
    rim_cells = cycle_strips(spread).astype(jnp.bfloat16)
    all_rims = lax.all_gather(rim_cells[None], "tile", axis=0, tiled=True)
    incoming = pick_gathered(all_rims, near_tiles, facing, flipped, usable)
    input_grad = absorb_rims(spread[:, 1:-1, 1:-1], incoming.astype(jnp.float32)).astype(
        jnp.bfloat16
    )
    input_grad = input_grad.reshape(cotangent.shape)
    cells = dp_count * sample_count * tiles * side * side
    grad = summed_grad * (1.0 / math.sqrt(cells))
    rows_per = left_factor.shape[0]
    width = left_factor.shape[1]
    cols_per = left_basis.shape[1]
    col_start = dp_index * cols_per
    grad_rows = lax.dynamic_slice_in_dim(grad, tile_index * rows_per, rows_per, 0)
    left_new = 0.95 * left_factor + 0.05 * lax.dot_general(
        grad_rows, grad, (((1,), (1,)), ((), ())), precision=highest
    )
    basis_rows = lax.all_gather(left_basis, "dp", axis=1, tiled=True)
    power = jnp.zeros((rows_per, width), jnp.float32) + jnp.dot(
        left_new,
        lax.all_gather(basis_rows.astype(jnp.bfloat16), "tile", axis=0, tiled=True).astype(
            jnp.float32
        ),
        precision=highest,
    )
    power_cols = lax.dynamic_slice_in_dim(power, col_start, cols_per, 1)
    gram_part = lax.psum(
        lax.dot_general(power, power_cols, (((0,), (0,)), ((), ())), precision=highest), "tile"
    )
    gram = lax.all_gather(gram_part, "dp", axis=1, tiled=True)
    lower = jnp.linalg.cholesky(gram)
    basis_new = lax.linalg.triangular_solve(lower, power.T, left_side=True, lower=True).T
    right_new = 0.95 * right_factor + 0.05 * lax.dot_general(
        grad, grad, (((0,), (0,)), ((), ())), precision=highest
    )
    right_basis_new = orthonormal(jnp.dot(right_new, right_basis, precision=highest))
    back = lax.psum(jnp.dot(left_basis, momentum, precision=highest), "dp")
    basis_cols = lax.dynamic_slice_in_dim(basis_new, col_start, cols_per, 1)
    turned_momentum, turned_grad = lax.psum(
        (
            lax.dot_general(basis_cols, back, (((0,), (0,)), ((), ())), precision=highest),
            lax.dot_general(basis_cols, grad_rows, (((0,), (0,)), ((), ())), precision=highest),
        ),
        "tile",
    )
    right_turn = lax.dot_general(
        right_basis, right_basis_new, (((0,), (0,)), ((), ())), precision=highest
    )
    rotated = jnp.dot(turned_momentum, right_turn, precision=highest)
    projected = jnp.dot(turned_grad, right_basis_new, precision=highest)
    momentum_new = 0.9 * rotated + 0.1 * projected
    second_new = 0.95 * second_moment + 0.05 * projected * projected
    normalized = momentum_new / (jnp.sqrt(second_new) + epsilon)
    whole_moment = lax.all_gather(normalized, "dp", axis=0, tiled=True)
    update_rows = jnp.dot(basis_new, whole_moment, precision=highest)
    update = lax.dot_general(
        update_rows, right_basis_new, (((1,), (1,)), ((), ())), precision=highest
    )
    return (
        result,
        input_grad,
        grad,
        left_new,
        basis_new,
        right_new,
        right_basis_new,
        momentum_new,
        second_new,
        update,
    )


def solution(mesh):
    placed = (
        P(("group", "dp"), "tile", None, None, None),
        P(("group", "dp"), "tile", None, None, None),
        P("group", None),
        P("tile"),
        P("tile", None),
        P(("group", "tile"), None),
        P(("group", "tile"), "dp"),
        P("group", None),
        P("group", None),
        P(("group", "dp"), None),
        P(("group", "dp"), None),
    )
    return jax.shard_map(
        body,
        mesh=mesh,
        in_specs=placed,
        out_specs=(
            P(("group", "dp"), "tile", None, None, None),
            P(("group", "dp"), "tile", None, None, None),
            P("group", None),
            P(("group", "tile"), None),
            P(("group", "tile"), None),
            P("group", None),
            P("group", None),
            P(("group", "dp"), None),
            P(("group", "dp"), None),
            P(("group", "tile"), None),
        ),
        check_vma=False,
    )
```

profile of v0, /device:TPU:0, one launch (start us, length us, event | category | flops | bytes accessed | tf_op | source)
XLA Modules:
  0.0 795.9 jit_solution(18225096363000132094)
XLA Ops:
  19.2 15.8 %all_gather.19 = bf16[8,4,1,24,128]{4,3,2,1,0:T(8,128)(2,1)S(1)} all-gather(bf16[1,4,1,24,128]{4,3,2,1,0:T(8,128)(2,1)S(1)} %pad_maximum_fusion.4), channel_id=1, replica_groups=mesh['group'=1,'tile'=8,'dp'=4] {'tile'}, dimensions={0}, use_global_device_ids=true | all-gather | bytes 221184 | tf_op jit(solution)/shard_map/all_gather | solution.py:143
  36.3 14.1 %all-gather = bf16[32,1,24,128]{3,2,1,0:T(8,128)(2,1)S(1)} all-gather(bf16[4,1,24,128]{3,2,1,0:T(8,128)(2,1)S(1)} %pad_maximum_fusion.3), channel_id=2, replica_groups=mesh['group'=1,'tile'=8,'dp'=4] {'tile'}, dimensions={0}, use_global_device_ids=true | all-gather | bytes 221184 | tf_op jit(solution)/shard_map/all_gather | solution.py:130
  53.1 10.2 %all-gather.1 = bf16[4,288,144]{1,2,0:T(8,128)(2,1)S(1)} all-gather(bf16[1,288,144]{1,2,0:T(8,128)(2,1)S(1)} %bitcast_convert_fusion), channel_id=1, replica_groups=mesh['group'=1,'tile'=8,'dp'=4] {'dp'}, dimensions={0}, use_global_device_ids=true | all-gather | bytes 414720 | tf_op jit(solution)/shard_map/all_gather | solution.py:159
  64.7 132.0 %all-reduce.18.cloned.1.call-done = f32[1152,128]{1,0:T(8,128)} async-done(((f32[1152,128]{1,0:T(8,128)}), f32[1152,128]{1,0:T(8,128)}) %all-reduce.18.cloned.1.call-update) | async-done | bytes 589840 | tf_op jit(solution)/shard_map/psum | solution.py:138
  206.1 60.6 %all-reduce.20.cloned.1.call-done = f32[1152,288]{0,1:T(8,128)} async-done(((f32[1152,288]{0,1:T(8,128)}), f32[1152,288]{0,1:T(8,128)}) %all-reduce.20.cloned.1.call-update) | async-done | bytes 1327120 | tf_op jit(solution)/shard_map/psum | solution.py:168
  276.5 11.7 %cholesky.693 = f32[128,128]{1,0:T(8,128)S(1)} custom-call(f32[128,128]{1,0:T(8,128)S(1)} %fusion.98), custom_call_target="Cholesky" | custom-call | tf_op jit(solution)/shard_map/jit(cholesky)/cholesky | solution.py:82
  289.6 9.8 %custom-call.85 = f32[1,128,128]{1,2,0:T(8,128)S(1)} custom-call(f32[1,128,128]{2,1,0:T(8,128)S(1)} %fusion.85), custom_call_target="InvertDiagBlocksLowerTriangular" | custom-call | tf_op jit(solution)/shard_map/triangular_solve | solution.py:83
  300.4 28.1 %all-gather.7.cloned.1.call-done = f32[1152,1152]{0,1:T(8,128)} async-done(((f32[1152,288]{0,1:T(8,128)}), f32[1152,1152]{0,1:T(8,128)}) %all-gather.7.cloned.1.call-update) | async-done | bytes 5308432 | tf_op jit(solution)/shard_map/all_gather | solution.py:171
  342.7 11.7 %cholesky.273 = f32[128,128]{1,0:T(8,128)S(1)} custom-call(f32[128,128]{1,0:T(8,128)S(1)} %cholesky.705), custom_call_target="Cholesky" | custom-call | tf_op jit(solution)/shard_map/jit(cholesky)/cholesky | solution.py:172
  357.1 9.8 %custom-call.76 = f32[1,128,128]{1,2,0:T(8,128)S(1)} custom-call(f32[1,128,128]{2,1,0:T(8,128)S(1)} %get-tuple-element.210), custom_call_target="InvertDiagBlocksLowerTriangular" | custom-call | tf_op jit(solution)/shard_map/jit(cholesky)/cholesky | solution.py:172
  371.1 11.7 %cholesky.294 = f32[128,128]{1,0:T(8,128)S(1)} custom-call(f32[128,128]{1,0:T(8,128)S(1)} %cholesky.709), custom_call_target="Cholesky" | custom-call | tf_op jit(solution)/shard_map/jit(cholesky)/cholesky | solution.py:172
  383.5 10.0 %custom-call.77 = f32[1,128,128]{1,2,0:T(8,128)S(1)} custom-call(f32[1,128,128]{2,1,0:T(8,128)S(1)} %get-tuple-element.207), custom_call_target="InvertDiagBlocksLowerTriangular" | custom-call | tf_op jit(solution)/shard_map/jit(cholesky)/cholesky | solution.py:172
  397.1 11.7 %cholesky.321 = f32[128,128]{1,0:T(8,128)S(1)} custom-call(f32[128,128]{1,0:T(8,128)S(1)} %cholesky.714), custom_call_target="Cholesky" | custom-call | tf_op jit(solution)/shard_map/jit(cholesky)/cholesky | solution.py:172
  423.2 11.9 %cholesky.583 = f32[128,128]{1,0:T(8,128)S(1)} custom-call(f32[128,128]{1,0:T(8,128)S(1)} %cholesky.719), custom_call_target="Cholesky" | custom-call | tf_op jit(solution)/shard_map/jit(cholesky)/cholesky | solution.py:172
  449.3 11.7 %cholesky.602 = f32[128,128]{1,0:T(8,128)S(1)} custom-call(f32[128,128]{1,0:T(8,128)S(1)} %cholesky.724), custom_call_target="Cholesky" | custom-call | tf_op jit(solution)/shard_map/jit(cholesky)/cholesky | solution.py:172
  461.7 10.2 %custom-call.80 = f32[1,128,128]{1,2,0:T(8,128)S(1)} custom-call(f32[1,128,128]{2,1,0:T(8,128)S(1)} %get-tuple-element.198), custom_call_target="InvertDiagBlocksLowerTriangular" | custom-call | tf_op jit(solution)/shard_map/jit(cholesky)/cholesky | solution.py:172
  475.8 11.7 %cholesky.622 = f32[128,128]{1,0:T(8,128)S(1)} custom-call(f32[128,128]{1,0:T(8,128)S(1)} %cholesky.729), custom_call_target="Cholesky" | custom-call | tf_op jit(solution)/shard_map/jit(cholesky)/cholesky | solution.py:172
  501.6 11.9 %cholesky.642 = f32[128,128]{1,0:T(8,128)S(1)} custom-call(f32[128,128]{1,0:T(8,128)S(1)} %cholesky.734), custom_call_target="Cholesky" | custom-call | tf_op jit(solution)/shard_map/jit(cholesky)/cholesky | solution.py:172
  527.1 11.7 %cholesky.662 = f32[128,128]{1,0:T(8,128)S(1)} custom-call(f32[128,128]{1,0:T(8,128)S(1)} %cholesky.739), custom_call_target="Cholesky" | custom-call | tf_op jit(solution)/shard_map/jit(cholesky)/cholesky | solution.py:172
  551.9 11.9 %cholesky.680 = f32[128,128]{1,0:T(8,128)S(1)} custom-call(f32[128,128]{1,0:T(8,128)S(1)} %convolution_subtract_fusion.12), custom_call_target="Cholesky" | custom-call | tf_op jit(solution)/shard_map/jit(cholesky)/cholesky | solution.py:172
  581.3 31.4 %while.5 = (s32[]{:T(128)}, f32[1152,1152]{1,0:T(8,128)}, s32[9,2]{0,1:T(2,128)S(1)}, f32[9,128,128]{2,1,0:T(8,128)}, s32[]{:T(128)}) while((s32[]{:T(128)}, f32[1152,1152]{1,0:T(8,128)}, s32[9,2]{0,1:T(2,128)S(1)}, f32[9,128,128]{2,1,0:T(8,128)}, s32[]{:T(128)}) %tuple.112), condition=%wide.while_cond.4, body=%wide.while_body.4.sunk | while | flops 2 | bytes 132205 | solution.py:173
  612.8 89.2 %custom-call.84 = f32[9,128,128]{1,2,0:T(8,128)S(1)} custom-call(f32[9,128,128]{2,1,0:T(8,128)} %get-tuple-element.65), custom_call_target="InvertDiagBlocksLowerTriangular" | custom-call | tf_op jit(solution)/shard_map/triangular_solve | solution.py:173
  719.5 52.8 %all-reduce.24.cloned.1.call-done = (f32[288,128]{1,0:T(8,128)}, f32[288,128]{1,0:T(8,128)}) async-done(((f32[288,128]{1,0:T(8,128)}, f32[288,128]{1,0:T(8,128)}), (f32[288,128]{1,0:T(8,128)}, f32[288,128]{1,0:T(8,128)})) %all-reduce.24.cloned.1.call-update) | async-done | bytes 294928 | tf_op jit(solution)/shard_map/psum | solution.py:180
  775.4 11.2 %all_gather.23 = f32[1152,128]{1,0:T(8,128)S(1)} all-gather(f32[288,128]{1,0:T(8,128)S(1)} %get-tuple-element.128), channel_id=1, replica_groups=mesh['group'=1,'tile'=8,'dp'=4] {'dp'}, dimensions={0}, use_global_device_ids=true | all-gather | bytes 737280 | tf_op jit(solution)/shard_map/all_gather | solution.py:195
  (221 shorter events, 201.5 us)
Async XLA Ops:
  8.0 1.0 copy-start
  8.0 27.8 %copy-start.11 = (s32[4]{0:T(128)S(1)}, s32[4]{0:T(128)}, u32[]{:S(2)}) copy-start(s32[4]{0:T(128)} %constant.530.clone) | copy-start | bytes 52
  8.0 11.1 %copy-start.5 = (bf16[1,1,24,24,128]{4,3,2,1,0:T(8,128)(2,1)S(1)}, bf16[1,1,24,24,128]{4,3,2,1,0:T(8,128)(2,1)}, u32[]{:S(2)}) copy-start(bf16[1,1,24,24,128]{4,3,2,1,0:T(8,128)(2,1)} %param.20) | copy-start | bytes 442372
  8.0 27.6 %copy-start.10 = (s32[1,4]{1,0:T(1,128)S(1)}, s32[1,4]{1,0:T(1,128)}, u32[]{:S(2)}) copy-start(s32[1,4]{1,0:T(1,128)} %param.24) | copy-start | bytes 52
  8.1 188.6 %all-reduce.18.cloned.1.call-start = ((), (), s32[]{:S(2)}) async-start(), calls=%async_computation | async-start | bytes 1179648 | tf_op jit(solution)/shard_map/psum | solution.py:138
  19.0 34.1 %copy-start.6 = (f32[144,288]{1,0:T(8,128)S(1)}, f32[144,288]{1,0:T(8,128)}, u32[]{:S(2)}) copy-start(f32[144,288]{1,0:T(8,128)} %param.26) | copy-start | bytes 497668
  53.1 146.8 %all-gather.5.cloned.1.call-start = ((), (), s32[]{:S(2)}) async-start(), calls=%async_computation.1 | async-start | bytes 2985984 | tf_op jit(solution)/shard_map/all_gather | solution.py:162
  64.6 202.1 %all-reduce.20.cloned.1.call-start = ((), (), s32[]{:S(2)}) async-start(), calls=%async_computation.2 | async-start | bytes 2654208 | tf_op jit(solution)/shard_map/psum | solution.py:168
  197.8 517.7 %copy-start.2 = (f32[1152,128]{1,0:T(8,128)}, f32[1152,128]{1,0:T(8,128)S(1)}, u32[]{:S(2)}) copy-start(f32[1152,128]{1,0:T(8,128)S(1)} %broadcast_multiply_fusion) | copy-start | bytes 1769476
  199.8 71.1 %copy-start.3 = (f32[144,1152]{1,0:T(8,128)}, f32[144,1152]{1,0:T(8,128)S(1)}, u32[]{:S(2)}) copy-start(f32[144,1152]{1,0:T(8,128)S(1)} %fusion.1) | copy-start | bytes 1990660
  203.4 72.4 %copy-start.7 = (f32[128,128]{1,0:T(8,128)S(1)}, f32[128,128]{1,0:T(8,128)}, u32[]{:S(2)}) copy-start(f32[128,128]{1,0:T(8,128)} %param.28) | copy-start | bytes 196612
  206.0 122.4 %all-gather.7.cloned.1.call-start = ((), (), s32[]{:S(2)}) async-start(), calls=%async_computation.3 | async-start | bytes 6635520 | tf_op jit(solution)/shard_map/all_gather | solution.py:171
  266.7 450.2 %all-reduce.22.cloned.1.call-start = ((), (), s32[]{:S(2)}) async-start(), calls=%async_computation.4 | async-start | bytes 147456 | tf_op jit(solution)/shard_map/psum | solution.py:178
  268.7 503.5 %all-reduce.24.cloned.1.call-start = ((), (), s32[]{:S(2)}) async-start(), calls=%async_computation.5 | async-start | bytes 589824 | tf_op jit(solution)/shard_map/psum | solution.py:180
  275.9 59.8 %copy-start.8 = (f32[128,128]{1,0:T(8,128)}, f32[128,128]{1,0:T(8,128)S(1)}, u32[]{:S(2)}) copy-start(f32[128,128]{1,0:T(8,128)S(1)} %fusion.19) | copy-start | bytes 196612
  340.4 2.3 copy-start.1
  703.6 69.9 %copy-start.9 = (f32[288,128]{1,0:T(8,128)S(1)}, f32[288,128]{1,0:T(8,128)}, u32[]{:S(2)}) copy-start(f32[288,128]{1,0:T(8,128)} %param.30) | copy-start | bytes 442372
  715.4 72.7 %copy-start.4 = (f32[1152,144]{0,1:T(8,128)}, f32[1152,144]{0,1:T(8,128)S(1)}, u32[]{:S(2)}) copy-start(f32[1152,144]{0,1:T(8,128)S(1)} %convolution_dynamic-update-slice_fusion.6) | copy-start | bytes 1990660
Sparse Core Ops, SparseCore 0:
  53.2 143.4 all-reduce.17
  266.8 61.6 all-gather.6
  331.9 40.6 all-reduce.21
Sparse Core Ops, SparseCore 1:
  64.7 35.0 all-gather.4
  206.1 60.5 all-reduce.19
  719.4 52.8 all-reduce.23
where the time goes:
time: 806 us; the launch traced here: 796 us
  other arithmetic  322 us (40%)
  waiting for transfers between devices  273 us (34%)
  matrix products  76.5 us (9%)
  blocking collectives  51.3 us (6%)
  local copies, waits for them, and re-layouts  49.5 us (6%)
  between operations  23.1 us (3%)
    another operation x35, other arithmetic, body(): lower = jnp.linalg.cholesky(gram)  196 us
    psum x1, waiting for transfers between devices, body(): summed_grad = lax.psum(partial_grad, ('tile', 'dp'))  132 us
    another operation x3, other arithmetic, body(): lax.linalg.triangular_solve(lower, power.T, left_side=True, lower=True)  94.4 us
    psum x1, waiting for transfers between devices, body(): lax.psum(lax.dot_general(power, power_cols, (((0,), (0,)), ((), ())), pre...  60.6 us
    psum x1, waiting for transfers between devices, body(): lax.psum((lax.dot_general(basis_cols, back, (((0,), (0,)), ((), ())), pre...  52.8 us
    another operation x27, local copies, waits for them, and re-layouts  31.4 us
    another operation x16, matrix products, body(): lower = jnp.linalg.cholesky(gram)  28.7 us
    all_gather x1, waiting for transfers between devices, body(): gram = lax.all_gather(gram_part, 'dp', axis=1, tiled=True)  28.1 us
  transfers between devices with their start and end apart: 6, of which 4 were waited for; matrix products, arithmetic and copies ran while one was open for 53% of the time, Pallas kernels for 0%

commit v1 on v0

--- a/solution.py
+++ b/solution.py
@@ -6,6 +6,29 @@
 
 highest = lax.Precision.HIGHEST
 epsilon = 1e-08
+
+
+def turn_point_by_axis(in_array):
+    y, value_now, far_arr = (lax.axis_size("dp"), lax.axis_index("dp"), in_array.shape[1])
+    kept_rows = [(ix, (ix + 1) % y) for ix in range(y)]
+    grid = [(ix, (ix - 1) % y) for ix in range(y)]
+    local_next = jnp.zeros((*in_array.shape[:1], y * far_arr, *in_array.shape[2:]), in_array.dtype)
+    local_next = lax.dynamic_update_slice_in_dim(local_next, in_array, value_now * far_arr, axis=1)
+    r1 = t_next = in_array
+    right_arr = y // 2
+    j = 1
+    while j < right_arr + 1:
+        r1 = lax.ppermute(r1, "dp", kept_rows)
+        local_next = lax.dynamic_update_slice_in_dim(
+            local_next, r1, (value_now - j) % y * far_arr, axis=1
+        )
+        if j < y - right_arr:
+            t_next = lax.ppermute(t_next, "dp", grid)
+            local_next = lax.dynamic_update_slice_in_dim(
+                local_next, t_next, (value_now + j) % y * far_arr, axis=1
+            )
+        j += 1
+    return local_next
 
 
 def edge_strips(values):
@@ -168,7 +191,7 @@
     gram_part = lax.psum(
         lax.dot_general(power, power_cols, (((0,), (0,)), ((), ())), precision=highest), "tile"
     )
-    gram = lax.all_gather(gram_part, "dp", axis=1, tiled=True)
+    gram = turn_point_by_axis(gram_part)
     lower = jnp.linalg.cholesky(gram)
     basis_new = lax.linalg.triangular_solve(lower, power.T, left_side=True, lower=True).T
     right_new = 0.95 * right_factor + 0.05 * lax.dot_general(

time: 806 us -> 853 us (1.058)
  local copies, waits for them, and re-layouts: 49.5 us -> 72.9 us
  matrix products: 76.5 us -> 89.8 us
    ppermute x0 -> x3, waiting for transfers between devices: none -> 48.2 us  [the longest x2 38.2 us: turn_point_by_axis(): r1 = lax.ppermute(r1, 'dp', kept_rows)]
    all_gather x1 -> x0, waiting for transfers between devices: 28.1 us -> none  [body(): gram = lax.all_gather(gram_part, 'dp', axis=1, tiled=True)]
    dynamic_update_slice x0 -> x5, local copies, waits for them, and re-layouts: none -> 15.8 us  [the longest x3 12.2 us: turn_point_by_axis(): lax.dynamic_update_slice_in_dim(local_next, r1, (value_now - j) % y * far...]
    psum x1, waiting for transfers between devices: 60.6 us -> 47.4 us  [body(): lax.psum(lax.dot_general(power, power_cols, (((0,), (0,)), ((), ())), pre...]
    another operation x27 -> x45, local copies, waits for them, and re-layouts: 31.4 us -> 32.3 us
  transfers between devices with their start and end apart: 6 -> 8, of which waited for: 4 -> 6; matrix products, arithmetic and copies ran while one was open for 53% -> 54% of each run, Pallas kernels for 0% -> 0%
where the time goes in v1:
time: 853 us; the launch traced here: 843 us
  other arithmetic  322 us (38%)
  waiting for transfers between devices  279 us (33%)
  matrix products  89.8 us (11%)
  local copies, waits for them, and re-layouts  72.9 us (9%)
  blocking collectives  51.3 us (6%)
  between operations  23.5 us (3%)
    another operation x35, other arithmetic, body(): lower = jnp.linalg.cholesky(gram)  191 us
    psum x1, waiting for transfers between devices, body(): summed_grad = lax.psum(partial_grad, ('tile', 'dp'))  132 us
    another operation x3, other arithmetic, body(): lax.linalg.triangular_solve(lower, power.T, left_side=True, lower=True)  95.3 us
    psum x1, waiting for transfers between devices, body(): lax.psum((lax.dot_general(basis_cols, back, (((0,), (0,)), ((), ())), pre...  51.2 us
    psum x1, waiting for transfers between devices, body(): lax.psum(lax.dot_general(power, power_cols, (((0,), (0,)), ((), ())), pre...  47.4 us
    ppermute x2, waiting for transfers between devices, turn_point_by_axis(): r1 = lax.ppermute(r1, 'dp', kept_rows)  38.2 us
    another operation x16, matrix products, body(): lower = jnp.linalg.cholesky(gram)  34.4 us
    another operation x45, local copies, waits for them, and re-layouts  32.3 us
  transfers between devices with their start and end apart: 8, of which 6 were waited for; matrix products, arithmetic and copies ran while one was open for 54% of the time, Pallas kernels for 0%

profile of v1, /device:TPU:0, one launch (start us, length us, event | category | flops | bytes accessed | tf_op | source)
XLA Modules:
  0.0 842.7 jit_solution(18357557804776997509)
XLA Ops:
  19.2 15.8 %all_gather.16 = bf16[8,4,1,24,128]{4,3,2,1,0:T(8,128)(2,1)S(1)} all-gather(bf16[1,4,1,24,128]{4,3,2,1,0:T(8,128)(2,1)S(1)} %pad_maximum_fusion.4), channel_id=1, replica_groups=mesh['group'=1,'tile'=8,'dp'=4] {'tile'}, dimensions={0}, use_global_device_ids=true | all-gather | bytes 221184 | tf_op jit(solution)/shard_map/all_gather | solution.py:166
  36.3 14.1 %all-gather = bf16[32,1,24,128]{3,2,1,0:T(8,128)(2,1)S(1)} all-gather(bf16[4,1,24,128]{3,2,1,0:T(8,128)(2,1)S(1)} %pad_maximum_fusion.3), channel_id=2, replica_groups=mesh['group'=1,'tile'=8,'dp'=4] {'tile'}, dimensions={0}, use_global_device_ids=true | all-gather | bytes 221184 | tf_op jit(solution)/shard_map/all_gather | solution.py:153
  53.8 10.2 %all-gather.1 = bf16[4,288,144]{1,2,0:T(8,128)(2,1)S(1)} all-gather(bf16[1,288,144]{1,2,0:T(8,128)(2,1)S(1)} %bitcast_convert_fusion), channel_id=1, replica_groups=mesh['group'=1,'tile'=8,'dp'=4] {'dp'}, dimensions={0}, use_global_device_ids=true | all-gather | bytes 414720 | tf_op jit(solution)/shard_map/all_gather | solution.py:182
  65.3 132.3 %all-reduce.18.cloned.1.call-done = f32[1152,128]{1,0:T(8,128)} async-done(((f32[1152,128]{1,0:T(8,128)}), f32[1152,128]{1,0:T(8,128)}) %all-reduce.18.cloned.1.call-update) | async-done | bytes 589840 | tf_op jit(solution)/shard_map/psum | solution.py:161
  220.1 47.4 %all-reduce.20.cloned.1.call-done = f32[1152,288]{0,1:T(8,128)} async-done(((f32[1152,288]{0,1:T(8,128)}), f32[1152,288]{0,1:T(8,128)}) %all-reduce.20.cloned.1.call-update) | async-done | bytes 1327120 | tf_op jit(solution)/shard_map/psum | solution.py:191
  275.9 11.7 %cholesky.690 = f32[128,128]{1,0:T(8,128)S(1)} custom-call(f32[128,128]{1,0:T(8,128)S(1)} %fusion.108), custom_call_target="Cholesky" | custom-call | tf_op jit(solution)/shard_map/jit(cholesky)/cholesky | solution.py:105
  287.7 14.4 %collective-permute-done = f32[1152,288]{0,1:T(8,128)} collective-permute-done((f32[1152,288]{0,1:T(8,128)}, f32[1152,288]{0,1:T(8,128)}, u32[]{:S(2)}, u32[]{:S(2)}) %collective-permute-start) | collective-permute-done | bytes 1327136 | tf_op jit(solution)/shard_map/ppermute | solution.py:21
  303.7 9.8 %custom-call.85 = f32[1,128,128]{1,2,0:T(8,128)S(1)} custom-call(f32[1,128,128]{2,1,0:T(8,128)S(1)} %fusion.92), custom_call_target="InvertDiagBlocksLowerTriangular" | custom-call | tf_op jit(solution)/shard_map/triangular_solve | solution.py:106
  320.9 10.0 %collective-permute-done.1 = f32[1152,288]{0,1:T(8,128)} collective-permute-done((f32[1152,288]{0,1:T(8,128)}, f32[1152,288]{0,1:T(8,128)}, u32[]{:S(2)}, u32[]{:S(2)}) %collective-permute-start.1) | collective-permute-done | bytes 1327136 | tf_op jit(solution)/shard_map/ppermute | solution.py:26
  333.3 23.8 %collective-permute-done.2 = f32[1152,288]{0,1:T(8,128)} collective-permute-done((f32[1152,288]{0,1:T(8,128)}, f32[1152,288]{0,1:T(8,128)}, u32[]{:S(2)}, u32[]{:S(2)}) %collective-permute-start.2) | collective-permute-done | bytes 1327136 | tf_op jit(solution)/shard_map/ppermute | solution.py:21
  373.8 11.7 %cholesky.272 = f32[128,128]{1,0:T(8,128)S(1)} custom-call(f32[128,128]{1,0:T(8,128)S(1)} %cholesky.702), custom_call_target="Cholesky" | custom-call | tf_op jit(solution)/shard_map/jit(cholesky)/cholesky | solution.py:195
  385.7 9.8 %custom-call.76 = f32[1,128,128]{1,2,0:T(8,128)S(1)} custom-call(f32[1,128,128]{2,1,0:T(8,128)S(1)} %get-tuple-element.221), custom_call_target="InvertDiagBlocksLowerTriangular" | custom-call | tf_op jit(solution)/shard_map/jit(cholesky)/cholesky | solution.py:195
  399.0 11.7 %cholesky.293 = f32[128,128]{1,0:T(8,128)S(1)} custom-call(f32[128,128]{1,0:T(8,128)S(1)} %cholesky.706), custom_call_target="Cholesky" | custom-call | tf_op jit(solution)/shard_map/jit(cholesky)/cholesky | solution.py:195
  429.4 11.7 %cholesky.320 = f32[128,128]{1,0:T(8,128)S(1)} custom-call(f32[128,128]{1,0:T(8,128)S(1)} %cholesky.711), custom_call_target="Cholesky" | custom-call | tf_op jit(solution)/shard_map/jit(cholesky)/cholesky | solution.py:195
  456.8 11.7 %cholesky.581 = f32[128,128]{1,0:T(8,128)S(1)} custom-call(f32[128,128]{1,0:T(8,128)S(1)} %cholesky.716), custom_call_target="Cholesky" | custom-call | tf_op jit(solution)/shard_map/jit(cholesky)/cholesky | solution.py:195
  484.1 12.1 %cholesky.600 = f32[128,128]{1,0:T(8,128)S(1)} custom-call(f32[128,128]{1,0:T(8,128)S(1)} %cholesky.721), custom_call_target="Cholesky" | custom-call | tf_op jit(solution)/shard_map/jit(cholesky)/cholesky | solution.py:195
  511.7 11.7 %cholesky.620 = f32[128,128]{1,0:T(8,128)S(1)} custom-call(f32[128,128]{1,0:T(8,128)S(1)} %cholesky.726), custom_call_target="Cholesky" | custom-call | tf_op jit(solution)/shard_map/jit(cholesky)/cholesky | solution.py:195
  538.8 11.7 %cholesky.640 = f32[128,128]{1,0:T(8,128)S(1)} custom-call(f32[128,128]{1,0:T(8,128)S(1)} %cholesky.731), custom_call_target="Cholesky" | custom-call | tf_op jit(solution)/shard_map/jit(cholesky)/cholesky | solution.py:195
  565.1 11.9 %cholesky.660 = f32[128,128]{1,0:T(8,128)S(1)} custom-call(f32[128,128]{1,0:T(8,128)S(1)} %cholesky.736), custom_call_target="Cholesky" | custom-call | tf_op jit(solution)/shard_map/jit(cholesky)/cholesky | solution.py:195
  590.8 11.7 %cholesky.678 = f32[128,128]{1,0:T(8,128)S(1)} custom-call(f32[128,128]{1,0:T(8,128)S(1)} %slice_subtract_fusion.7), custom_call_target="Cholesky" | custom-call | tf_op jit(solution)/shard_map/jit(cholesky)/cholesky | solution.py:195
  620.1 32.4 %while.5 = (s32[]{:T(128)}, f32[1152,1152]{0,1:T(8,128)}, s32[9,2]{0,1:T(2,128)S(1)}, f32[9,128,128]{2,1,0:T(8,128)}, s32[]{:T(128)}) while((s32[]{:T(128)}, f32[1152,1152]{0,1:T(8,128)}, s32[9,2]{0,1:T(2,128)S(1)}, f32[9,128,128]{2,1,0:T(8,128)}, s32[]{:T(128)}) %tuple.108), condition=%wide.while_cond.4, body=%wide.while_body.4.sunk | while | flops 2 | bytes 393329 | solution.py:196
  652.5 90.1 %custom-call.84 = f32[9,128,128]{1,2,0:T(8,128)} custom-call(f32[9,128,128]{2,1,0:T(8,128)} %get-tuple-element.65), custom_call_target="InvertDiagBlocksLowerTriangular" | custom-call | tf_op jit(solution)/shard_map/triangular_solve | solution.py:196
  767.6 51.2 %all-reduce.24.cloned.1.call-done = (f32[288,128]{1,0:T(8,128)}, f32[288,128]{1,0:T(8,128)}) async-done(((f32[288,128]{1,0:T(8,128)}, f32[288,128]{1,0:T(8,128)}), (f32[288,128]{1,0:T(8,128)}, f32[288,128]{1,0:T(8,128)})) %all-reduce.24.cloned.1.call-update) | async-done | bytes 294928 | tf_op jit(solution)/shard_map/psum | solution.py:203
  821.9 11.2 %all_gather.19 = f32[1152,128]{1,0:T(8,128)S(1)} all-gather(f32[288,128]{1,0:T(8,128)S(1)} %get-tuple-element.148), channel_id=1, replica_groups=mesh['group'=1,'tile'=8,'dp'=4] {'dp'}, dimensions={0}, use_global_device_ids=true | all-gather | bytes 737280 | tf_op jit(solution)/shard_map/all_gather | solution.py:218
  (272 shorter events, 261.4 us)
Async XLA Ops:
  8.0 1.0 copy-start
  8.0 27.8 %copy-start.14 = (s32[4]{0:T(128)S(1)}, s32[4]{0:T(128)}, u32[]{:S(2)}) copy-start(s32[4]{0:T(128)} %constant.547.clone) | copy-start | bytes 52
  8.0 11.1 %copy-start.5 = (bf16[1,1,24,24,128]{4,3,2,1,0:T(8,128)(2,1)S(1)}, bf16[1,1,24,24,128]{4,3,2,1,0:T(8,128)(2,1)}, u32[]{:S(2)}) copy-start(bf16[1,1,24,24,128]{4,3,2,1,0:T(8,128)(2,1)} %param.20) | copy-start | bytes 442372
  8.0 27.6 %copy-start.13 = (s32[1,4]{1,0:T(1,128)S(1)}, s32[1,4]{1,0:T(1,128)}, u32[]{:S(2)}) copy-start(s32[1,4]{1,0:T(1,128)} %param.24) | copy-start | bytes 52
  8.1 189.5 %all-reduce.18.cloned.1.call-start = ((), (), s32[]{:S(2)}) async-start(), calls=%async_computation | async-start | bytes 1179648 | tf_op jit(solution)/shard_map/psum | solution.py:161
  19.1 34.7 %copy-start.7 = (f32[144,288]{1,0:T(8,128)S(1)}, f32[144,288]{1,0:T(8,128)}, u32[]{:S(2)}) copy-start(f32[144,288]{1,0:T(8,128)} %param.26) | copy-start | bytes 497668
  53.7 147.1 %all-gather.4.cloned.1.call-start = ((), (), s32[]{:S(2)}) async-start(), calls=%async_computation.1 | async-start | bytes 2985984 | tf_op jit(solution)/shard_map/all_gather | solution.py:185
  65.2 202.3 %all-reduce.20.cloned.1.call-start = ((), (), s32[]{:S(2)}) async-start(), calls=%async_computation.2 | async-start | bytes 2654208 | tf_op jit(solution)/shard_map/psum | solution.py:191
  198.7 564.9 %copy-start.2 = (f32[1152,128]{1,0:T(8,128)}, f32[1152,128]{1,0:T(8,128)S(1)}, u32[]{:S(2)}) copy-start(f32[1152,128]{1,0:T(8,128)S(1)} %broadcast_multiply_fusion) | copy-start | bytes 1769476
  198.7 12.3 %copy-start.11 = (f32[4,1,24,128]{3,2,1,0:T(8,128)S(1)}, f32[4,1,24,128]{3,2,1,0:T(8,128)}, u32[]{:S(2)}) copy-start(f32[4,1,24,128]{3,2,1,0:T(8,128)} %get-tuple-element.228) | copy-start | bytes 147460
  200.8 70.6 %copy-start.3 = (f32[144,1152]{1,0:T(8,128)}, f32[144,1152]{1,0:T(8,128)S(1)}, u32[]{:S(2)}) copy-start(f32[144,1152]{1,0:T(8,128)S(1)} %fusion.1) | copy-start | bytes 1990660
  204.4 69.0 %copy-start.8 = (f32[128,128]{1,0:T(8,128)S(1)}, f32[128,128]{1,0:T(8,128)}, u32[]{:S(2)}) copy-start(f32[128,128]{1,0:T(8,128)} %param.28) | copy-start | bytes 196612
  207.0 558.1 %all-reduce.22.cloned.1.call-start = ((), (), s32[]{:S(2)}) async-start(), calls=%async_computation.3 | async-start | bytes 147456 | tf_op jit(solution)/shard_map/psum | solution.py:201
  209.0 609.8 %all-reduce.24.cloned.1.call-start = ((), (), s32[]{:S(2)}) async-start(), calls=%async_computation.4 | async-start | bytes 589824 | tf_op jit(solution)/shard_map/psum | solution.py:203
  267.5 34.6 %collective-permute-start = (f32[1152,288]{0,1:T(8,128)}, f32[1152,288]{0,1:T(8,128)}, u32[]{:S(2)}, u32[]{:S(2)}) collective-permute-start(f32[1152,288]{0,1:T(8,128)} %all-reduce.20.cloned.1.call-done), channel_id=1, source_target_pairs={{0,1},{1,2},{2,3},{3,0},{4,5},{5,6},{6,7},{7,4},{8,9},{9,10},{10,1... | collective-permute-start | bytes 3981320 | tf_op jit(solution)/shard_map/ppermute | solution.py:21
  271.3 45.9 %copy-start.6 = (f32[1152,288]{0,1:T(8,128)S(1)}, f32[1152,288]{0,1:T(8,128)}, u32[]{:S(2)}) copy-start(f32[1152,288]{0,1:T(8,128)} %all-reduce.20.cloned.1.call-done) | copy-start | bytes 3981316
  273.4 0.6 copy-start.10
  274.4 56.4 %collective-permute-start.1 = (f32[1152,288]{0,1:T(8,128)}, f32[1152,288]{0,1:T(8,128)}, u32[]{:S(2)}, u32[]{:S(2)}) collective-permute-start(f32[1152,288]{0,1:T(8,128)} %all-reduce.20.cloned.1.call-done), channel_id=1, source_target_pairs={{0,3},{1,0},{2,1},{3,2},{4,7},{5,4},{6,5},{7,6},{8,11},{9,8},{10,9... | collective-permute-start | bytes 3981320 | tf_op jit(solution)/shard_map/ppermute | solution.py:26
  302.1 55.1 %collective-permute-start.2 = (f32[1152,288]{0,1:T(8,128)}, f32[1152,288]{0,1:T(8,128)}, u32[]{:S(2)}, u32[]{:S(2)}) collective-permute-start(f32[1152,288]{0,1:T(8,128)} %collective-permute-done), channel_id=1, source_target_pairs={{0,1},{1,2},{2,3},{3,0},{4,5},{5,6},{6,7},{7,4},{8,9},{9,10},{10,1... | collective-permute-start | bytes 3981320 | tf_op jit(solution)/shard_map/ppermute | solution.py:21
  371.5 2.3 copy-start.1
  744.7 22.7 %copy-start.9 = (f32[128,128]{1,0:T(8,128)S(1)}, f32[128,128]{1,0:T(8,128)}, u32[]{:S(2)}) copy-start(f32[128,128]{1,0:T(8,128)} %param.28) | copy-start | bytes 196612
  745.8 74.2 %copy-start.12 = (f32[288,128]{1,0:T(8,128)S(1)}, f32[288,128]{1,0:T(8,128)}, u32[]{:S(2)}) copy-start(f32[288,128]{1,0:T(8,128)} %param.30) | copy-start | bytes 442372
  763.6 71.1 %copy-start.4 = (f32[1152,144]{0,1:T(8,128)}, f32[1152,144]{0,1:T(8,128)S(1)}, u32[]{:S(2)}) copy-start(f32[1152,144]{0,1:T(8,128)S(1)} %convolution_dynamic-update-slice_fusion.6) | copy-start | bytes 1990660
Sparse Core Ops, SparseCore 0:
  53.8 143.7 all-reduce.17
Sparse Core Ops, SparseCore 1:
  65.3 35.1 all-gather.3
  207.0 60.4 all-reduce.19
  270.9 40.9 all-reduce.21
  767.5 51.2 all-reduce.23
